TPU v7x, 256 devices: a whole 4x4x8 slice. The times are simulated.
256 devices in a mesh: tm: 8 (over z), row: 8 (over x, core), obs: 4 (over y).
Axes of the slice: x: 4, y: 4, z: 8, core: 2. Of those that a mesh axis runs over, the one named last changes fastest.
Arguments:
- dyn_pattern: int32 [16, 8, 3], P('tm'), may hold values from 0 to 7
- dyn_values: float32 [16, 1024, 384], P('tm', ('row', 'obs')), may hold values from -0.3125 to 0.3125
- offsets: float32 [16, 1024], P('tm', ('row', 'obs')), may hold values from -6 to 6
- covariance: float32 [16, 1024, 1024], P('tm', ('row', 'obs')), may hold values from -1 to 14, as said below
- obs_block: int32 [16, 128], P('tm'), may hold values from 0 to 7
- obs_matrix: float32 [16, 128, 256], P('tm', 'obs'), may hold values from -0.375 to 0.375
- obs_data: float32 [16, 128], P('tm', 'obs'), may hold values from -6 to 6
Outputs:
- scan_dynamics: float32 [8, 1024, 1024], P('tm', ('row', 'obs'))
- scan_offset: float32 [8, 1024], P('tm', ('row', 'obs'))
- scan_covariance: float32 [8, 1024, 1024], P('tm', ('row', 'obs'))
- scan_factor: float32 [8, 1024, 512], P('tm', ('row', 'obs'))
- scan_information: float32 [8, 1024], P('tm', ('row', 'obs'))
Inputs may be any that keep to these rules, and one draw needn't show every extreme that they name: `dyn_pattern`: each entry names a block column. `obs_block`: each entry names a state block. Each covariance is symmetric and positive definite.
All inputs are finite; a program needn't handle non-finite values.
Results may differ from a plain program's by a relative error of at most 0.00019.
Values sent between devices are 32-bit elements; how exact they have to be, the bound alone decides.
A program may use at most 128 MiB of HBM per device.

v0:
```python
import jax
import jax.numpy as jnp
from jax import lax
from jax.sharding import PartitionSpec as P

largest_value = lax.Precision.HIGHEST


def shifted(block, axis, distance):
    devices = range(lax.axis_size(axis))
    route = [(i - distance, i) for i in devices if i - distance in devices]
    return lax.ppermute(block, axis, route)


def product(left, right):
    return jnp.dot(left, right, precision=largest_value, preferred_element_type=jnp.float32)


def lower_solve(lower, rhs):
    return lax.linalg.triangular_solve(lower, rhs, left_side=True, lower=True)


def assemble_dynamics(pattern, values):
    number_of_blocks = pattern.shape[0]
    per_row = pattern.shape[1]
    states = values.shape[0]
    block_extent = states // number_of_blocks
    indicator_matrix = (
        pattern[:, :, None] == jnp.arange(number_of_blocks, dtype=jnp.int32)[None, None, :]
    ).astype(jnp.float32)
    blocks = values.reshape(number_of_blocks, block_extent, per_row, block_extent)
    return jnp.einsum("ckd,cikj->cidj", indicator_matrix, blocks, precision=largest_value).reshape(
        states, states
    )


def assemble_factor(indices, matrix, number_of_blocks):
    item_count = matrix.shape[0]
    block_extent = matrix.shape[1] // 2
    reach = (indices[:, None] + jnp.arange(2, dtype=jnp.int32)[None, :]) % number_of_blocks
    indicator_matrix = (
        reach[:, :, None] == jnp.arange(number_of_blocks, dtype=jnp.int32)[None, None, :]
    ).astype(jnp.float32)
    piece_list = matrix.reshape(item_count, 2, block_extent)
    return jnp.einsum(
        "onr,onz->rzo", indicator_matrix, piece_list, precision=largest_value
    ).reshape(number_of_blocks * block_extent, item_count)


def combine(
    prior_dyn,
    prior_offsets,
    prior_cov,
    prior_factor,
    prior_zeta,
    own_dyn,
    own_offsets,
    own_cov,
    own_factor,
    own_zeta,
    row_start,
):
    panel_rows = prior_cov.shape[0]
    rank_width = own_factor.shape[1]
    own_pan = lax.dynamic_slice_in_dim(own_dyn, row_start, panel_rows, 0)
    gain_pan = product(prior_cov, own_factor)
    gain_rows = lax.all_gather(gain_pan, ("row", "obs"), axis=0, tiled=True)
    identity = jnp.eye(rank_width, dtype=jnp.float32)
    factor_pan = lax.dynamic_slice_in_dim(own_factor, row_start, panel_rows, 0)
    system = identity + lax.psum(product(factor_pan.T, gain_pan), ("row", "obs"))
    lower = jnp.linalg.cholesky(system)
    carried = product(own_dyn, gain_rows)
    observed = product(prior_dyn.T, own_factor)
    upper_part = lower_solve(lower, observed.T)
    weights = lower_solve(lower, carried.T).T
    weight_pan = lax.dynamic_slice_in_dim(weights, row_start, panel_rows, 0)
    spread_pan = product(prior_cov, own_dyn.T)
    moved = product(own_pan, lax.all_gather(spread_pan, ("row", "obs"), axis=0, tiled=True))
    new_dyn = product(own_pan, prior_dyn) - product(weight_pan, upper_part)
    new_cov = moved - product(weight_pan, weights.T) + own_cov
    residual = own_zeta - product(own_factor.T, prior_offsets)
    solved = lower_solve(lower, residual[:, None])[:, 0]
    new_offsets = product(own_pan, prior_offsets) + product(weight_pan, solved) + own_offsets
    upper_pan = lax.dynamic_slice_in_dim(upper_part, row_start, panel_rows, 1).T
    new_factor = jnp.concatenate([upper_pan, prior_factor], axis=1)
    new_zeta = jnp.concatenate([solved, prior_zeta])
    return (new_dyn, new_offsets, new_cov, new_factor, new_zeta)


def per_device(dyn_pattern, dyn_values, offsets, covariance, obs_block, obs_matrix, obs_data):
    panel_rows = covariance.shape[1]
    row_start = lax.axis_index(("row", "obs")) * panel_rows
    number_of_blocks = dyn_pattern.shape[1]
    obs_rows, obs_values = (
        lax.all_gather(obs_matrix, "obs", axis=1, tiled=True),
        lax.all_gather(obs_data, "obs", axis=1, tiled=True),
    )
    row_values, row_offsets = (
        lax.all_gather(dyn_values, ("row", "obs"), axis=1, tiled=True),
        lax.all_gather(offsets, ("row", "obs"), axis=1, tiled=True),
    )
    first_dyn = assemble_dynamics(dyn_pattern[0], row_values[0])
    second_dyn = assemble_dynamics(dyn_pattern[1], row_values[1])
    first_factor = assemble_factor(obs_block[0], obs_rows[0], number_of_blocks)
    second_factor = assemble_factor(obs_block[1], obs_rows[1], number_of_blocks)
    first_pan = lax.dynamic_slice_in_dim(first_factor, row_start, panel_rows, 0)
    dyn_pan, off_pan, cov_pan, fac_pan, zeta_full = combine(
        first_dyn,
        row_offsets[0],
        covariance[0],
        first_pan,
        obs_values[0],
        second_dyn,
        offsets[1],
        covariance[1],
        second_factor,
        obs_values[1],
        row_start,
    )
    later_pan, later_cov, later_off, later_fac, later_zeta = shifted(
        (dyn_pan, cov_pan, off_pan, fac_pan, zeta_full), "tm", -1
    )
    prior_full, later_full, later_factor, prior_offsets = (
        lax.all_gather(dyn_pan, ("row", "obs"), axis=0, tiled=True),
        lax.all_gather(later_pan, ("row", "obs"), axis=0, tiled=True),
        lax.all_gather(later_fac, ("row", "obs"), axis=0, tiled=True),
        lax.all_gather(off_pan, ("row", "obs"), axis=0, tiled=True),
    )
    top_dyn, top_off, top_cov, top_fac, top_zeta = combine(
        prior_full,
        prior_offsets,
        cov_pan,
        fac_pan,
        zeta_full,
        later_full,
        later_off,
        later_cov,
        later_factor,
        later_zeta,
        row_start,
    )
    even_turn = lax.axis_index("tm") % 2 == 0
    padded_fac = jnp.concatenate([fac_pan, jnp.zeros_like(fac_pan)], axis=1)
    padded_zeta = jnp.concatenate([zeta_full, jnp.zeros_like(zeta_full)])
    out_dyn = jnp.where(even_turn, top_dyn, dyn_pan)
    out_off = jnp.where(even_turn, top_off, off_pan)
    out_cov = jnp.where(even_turn, top_cov, cov_pan)
    out_fac = jnp.where(even_turn, top_fac, padded_fac)
    out_zeta = jnp.where(even_turn, top_zeta, padded_zeta)
    output_information = product(out_fac, out_zeta)
    return (out_dyn[None], out_off[None], out_cov[None], out_fac[None], output_information[None])


def solution(mesh):
    placed = (
        P("tm", None, None),
        P("tm", ("row", "obs"), None),
        P("tm", ("row", "obs")),
        P("tm", ("row", "obs"), None),
        P("tm", None),
        P("tm", "obs", None),
        P("tm", "obs"),
    )
    return jax.shard_map(
        per_device,
        mesh=mesh,
        in_specs=placed,
        out_specs=(
            P("tm", ("row", "obs"), None),
            P("tm", ("row", "obs")),
            P("tm", ("row", "obs"), None),
            P("tm", ("row", "obs"), None),
            P("tm", ("row", "obs")),
        ),
        check_vma=False,
    )
```

profile of v0, /device:TPU:1, one launch (start us, length us, event | category | flops | bytes accessed | tf_op | source)
XLA Modules:
  0.0 616.6 jit_solution(8064863237237655006)
XLA Ops:
  8.0 11.5 %all_gather.37 = f32[2,128,256]{2,1,0:T(8,128)S(1)} all-gather(f32[2,32,256]{2,1,0:T(8,128)} %param.16), channel_id=1, replica_groups=mesh['tm'=8,'row'=8,'obs'=4] {'obs'}, dimensions={1}, use_global_device_ids=true | all-gather | bytes 327680 | tf_op jit(solution)/shard_map/all_gather | solution.py:95
  24.0 40.9 %all-gather.10.cloned.1.call-done = f32[2,1024,384]{2,1,0:T(8,128)} async-done(((f32[2,32,384]{2,1,0:T(8,128)}), f32[2,1024,384]{2,1,0:T(8,128)}) %all-gather.10.cloned.1.call-update) | async-done | bytes 3145744 | tf_op jit(solution)/shard_map/all_gather | solution.py:99
  78.1 4.9 convolution_bitcast_fusion.1
  84.7 89.2 %all-reduce.5.cloned.1.call-done = f32[128,128]{1,0:T(8,128)} async-done(((f32[128,128]{1,0:T(8,128)}), f32[128,128]{1,0:T(8,128)}) %all-reduce.5.cloned.1.call-update) | async-done | bytes 65552 | tf_op jit(solution)/shard_map/psum | solution.py:70
  175.6 11.7 %cholesky.60 = f32[128,128]{1,0:T(8,128)S(1)} custom-call(f32[128,128]{1,0:T(8,128)S(1)} %fusion.77), custom_call_target="Cholesky" | custom-call | tf_op jit(solution)/shard_map/jit(cholesky)/cholesky | solution.py:71
  188.7 9.8 %custom-call.31 = f32[1,128,128]{1,2,0:T(8,128)S(1)} custom-call(f32[1,128,128]{2,1,0:T(8,128)S(1)} %fusion.55), custom_call_target="InvertDiagBlocksLowerTriangular" | custom-call | tf_op jit(solution)/shard_map/triangular_solve/custom-call.4 | solution.py:20
  200.7 4.3 fusion.107
  216.6 42.6 %all_gather.38 = f32[1024,128]{1,0:T(8,128)S(1)} all-gather(f32[32,128]{1,0:T(8,128)S(1)} %bitcast.273), channel_id=1, replica_groups=mesh['tm'=8,'row'=8,'obs'=4] {'row','obs'}, dimensions={0}, use_global_device_ids=true | all-gather | bytes 540672 | tf_op jit(solution)/shard_map/all_gather | solution.py:67
  262.6 4.8 fusion.133
  273.0 4.4 collective-permute-done
  278.9 4.8 fusion.52
  288.9 40.2 %all-gather = f32[32,32,2]{1,2,0:T(2,128)S(1)} all-gather(f32[1,32,2]{1,2,0:T(2,128)S(1)} %bitcast.282), channel_id=1, replica_groups=mesh['tm'=8,'row'=8,'obs'=4] {'row','obs'}, dimensions={0}, use_global_device_ids=true | all-gather | bytes 8448 | tf_op jit(solution)/shard_map/all_gather | solution.py:100
  329.1 5.2 all-gather.1
  335.7 6.7 %fusion.141 = f32[32,1024]{1,0:T(8,128)} fusion(f32[32,1024]{1,0:T(8,128)S(1)} %fusion.12, f32[1024,1024]{1,0:T(8,128)} %all-gather.12.cloned.1.call-done), kind=kOutput, calls=%fused_computation.205 | convolution fusion | flops 402653184 | bytes 4456448 | tf_op jit(solution)/shard_map/dot_general | solution.py:16
  348.2 63.2 %all-reduce.1 = f32[1024]{0:T(1024)S(1)} all-reduce(f32[1024]{0:T(1024)S(1)} %dynamic-update-slice.17), channel_id=1, replica_groups=mesh['tm'=8,'row'=8,'obs'=4] {'row','obs'}, use_global_device_ids=true, to_apply=%add.1 | all-reduce | flops 1024 | bytes 8192
  413.4 6.0 fusion.140
  419.4 80.5 %all-reduce.7.cloned.1.call-done = f32[256,256]{0,1:T(8,128)} async-done(((f32[256,256]{0,1:T(8,128)}), f32[256,256]{0,1:T(8,128)}) %all-reduce.7.cloned.1.call-update) | async-done | bytes 262160 | tf_op jit(solution)/shard_map/psum | solution.py:70
  502.0 11.7 %cholesky.115 = f32[128,128]{1,0:T(8,128)S(1)} custom-call(f32[128,128]{1,0:T(8,128)S(1)} %cholesky.141), custom_call_target="Cholesky" | custom-call | tf_op jit(solution)/shard_map/jit(cholesky)/cholesky | solution.py:71
  513.8 9.8 %custom-call.26 = f32[1,128,128]{1,2,0:T(8,128)S(1)} custom-call(f32[1,128,128]{2,1,0:T(8,128)S(1)} %get-tuple-element.62), custom_call_target="InvertDiagBlocksLowerTriangular" | custom-call | tf_op jit(solution)/shard_map/jit(cholesky)/cholesky | solution.py:71
  524.1 11.7 %cholesky.128 = f32[128,128]{1,0:T(8,128)S(1)} custom-call(f32[128,128]{1,0:T(8,128)S(1)} %convolution_subtract_fusion.3), custom_call_target="Cholesky" | custom-call | tf_op jit(solution)/shard_map/jit(cholesky)/cholesky | solution.py:71
  542.5 19.8 %custom-call.33 = f32[2,128,128]{1,2,0:T(8,128)S(1)} custom-call(f32[2,128,128]{2,1,0:T(8,128)S(1)} %get-tuple-element.29), custom_call_target="InvertDiagBlocksLowerTriangular" | custom-call | tf_op jit(solution)/shard_map/triangular_solve/custom-call.5 | solution.py:20
  566.5 9.2 %fusion.139 = f32[256,1024]{1,0:T(8,128)S(1)} fusion(f32[1024,256]{1,0:T(8,128)} %all-gather.20.cloned.1.call-done, f32[1024,1024]{1,0:T(8,128)} %all-gather.12.cloned.1.call-done), kind=kOutput, calls=%fused_computation.203 | convolution fusion | flops 3221225472 | bytes 6291456 | tf_op jit(solution)/shard_map/dot_general | solution.py:16
  585.1 19.4 %all-gather.22.cloned.1.call-done = f32[1024,1024]{1,0:T(8,128)} async-done(((f32[32,1024]{1,0:T(8,128)}), f32[1024,1024]{1,0:T(8,128)}) %all-gather.22.cloned.1.call-update) | async-done | bytes 4194320 | tf_op jit(solution)/shard_map/all_gather | solution.py:78
  604.5 5.4 fusion.11
  (167 shorter events, 86.2 us)
Async XLA Ops:
  7.2 16.8 %copy-start.15 = (s32[2,8,3]{1,0,2:T(2,128)S(1)}, s32[2,8,3]{1,0,2:T(2,128)}, u32[]{:S(2)}) copy-start(s32[2,8,3]{1,0,2:T(2,128)} %param.11) | copy-start | bytes 580
  7.2 57.8 %all-gather.10.cloned.1.call-start = ((), (), s32[]{:S(2)}) async-start(), calls=%async_computation | async-start | bytes 3244032 | tf_op jit(solution)/shard_map/all_gather | solution.py:99
  7.9 165.9 %all-reduce.5.cloned.1.call-start = ((), (), s32[]{:S(2)}) async-start(), calls=%async_computation.1 | async-start | bytes 131072 | tf_op jit(solution)/shard_map/psum | solution.py:70
  23.9 255.0 %all-gather.18.cloned.1.call-start = ((), (), s32[]{:S(2)}) async-start(), calls=%async_computation.5 | async-start | bytes 4325376 | tf_op jit(solution)/shard_map/all_gather | solution.py:78
  68.2 9.9 %copy-start.10 = (f32[2,32,1024]{2,1,0:T(8,128)S(1)}, f32[2,32,1024]{2,1,0:T(8,128)}, u32[]{:S(2)}) copy-start(f32[2,32,1024]{2,1,0:T(8,128)} %param.14) | copy-start | bytes 786436
  83.0 201.2 %all-gather.16.cloned.1.call-start = ((), (), s32[]{:S(2)}) async-start(), calls=%async_computation.4 | async-start | bytes 1081344 | tf_op jit(solution)/shard_map/all_gather | solution.py:126
  84.6 120.4 %copy-start.9 = (f32[8,128,128]{2,1,0:T(8,128)}, f32[8,128,128]{2,1,0:T(8,128)S(1)}, u32[]{:S(2)}) copy-start(f32[8,128,128]{2,1,0:T(8,128)S(1)} %copy.56) | copy-start | bytes 1572868
  210.9 5.0 collective-permute-start.1
  216.5 119.2 %all-gather.12.cloned.1.call-start = ((), (), s32[]{:S(2)}) async-start(), calls=%async_computation.2 | async-start | bytes 4325376 | tf_op jit(solution)/shard_map/all_gather | solution.py:125
  262.6 5.9 copy-start.6
  262.6 5.9 copy-start.3
  271.5 6.6 %copy-start.7 = (f32[32,1024]{1,0:T(8,128)}, f32[32,1024]{1,0:T(8,128)S(1)}, u32[]{:S(2)}) copy-start(f32[32,1024]{1,0:T(8,128)S(1)} %fusion.6) | copy-start | bytes 393220
  271.5 17.3 %copy-start.14 = (f32[2,32]{1,0:T(2,128)S(1)}, f32[2,32]{1,0:T(2,128)}, u32[]{:S(2)}) copy-start(f32[2,32]{1,0:T(2,128)} %param.13) | copy-start | bytes 772
  271.5 57.6 %copy-start.16 = (f32[2,32]{1,0:T(2,128)S(1)}, f32[2,32]{1,0:T(2,128)}, u32[]{:S(2)}) copy-start(f32[2,32]{1,0:T(2,128)} %param.17) | copy-start | bytes 772
  271.5 5.8 collective-permute-start
  278.1 135.3 %all-gather.14.cloned.1.call-start = ((), (), s32[]{:S(2)}) async-start(), calls=%async_computation.3 | async-start | bytes 4325376 | tf_op jit(solution)/shard_map/all_gather | solution.py:124
  278.6 221.2 %all-reduce.7.cloned.1.call-start = ((), (), s32[]{:S(2)}) async-start(), calls=%async_computation.6 | async-start | bytes 524288 | tf_op jit(solution)/shard_map/psum | solution.py:70
  283.7 58.8 %copy-start.17 = (u32[256]{0:T(256)S(1)}, u32[256]{0:T(256)}, u32[]{:S(2)}) copy-start(u32[256]{0:T(256)} %constant.217) | copy-start | bytes 3076
  284.2 127.2 %copy-start.5 = (f32[1024,256]{1,0:T(8,128)S(1)}, f32[1024,256]{1,0:T(8,128)}, u32[]{:S(2)}) copy-start(f32[1024,256]{1,0:T(8,128)} %all-gather.16.cloned.1.call-done) | copy-start | bytes 3145732
  288.1 278.4 %all-gather.20.cloned.1.call-start = ((), (), s32[]{:S(2)}) async-start(), calls=%async_computation.7 | async-start | bytes 1081344 | tf_op jit(solution)/shard_map/all_gather | solution.py:67
  288.8 315.7 %all-gather.22.cloned.1.call-start = ((), (), s32[]{:S(2)}) async-start(), calls=%async_computation.8 | async-start | bytes 4325376 | tf_op jit(solution)/shard_map/all_gather | solution.py:78
  343.9 68.2 %collective-permute-start.2 = (f32[256]{0:T(256)S(1)}, f32[256]{0:T(256)S(1)}, u32[]{:S(2)}, u32[]{:S(2)}) collective-permute-start(f32[256]{0:T(256)S(1)} %pad_maximum_fusion.5), channel_id=1, source_target_pairs={{32,0},{64,32},{96,64},{128,96},{160,128},{192,160},{224,192},{33,... | collective-permute-start | bytes 3080 | tf_op jit(solution)/shard_map/ppermute | solution.py:12
  346.6 236.8 %collective-permute-start.3 = (f32[32]{0:T(128)S(1)}, f32[32]{0:T(128)S(1)}, u32[]{:S(2)}, u32[]{:S(2)}) collective-permute-start(f32[32]{0:T(128)S(1)} %fusion.16), channel_id=1, source_target_pairs={{32,0},{64,32},{96,64},{128,96},{160,128},{192,160},{224,192},{33,... | collective-permute-start | bytes 392 | tf_op jit(solution)/shard_map/ppermute | solution.py:12
  412.1 173.0 %collective-permute-start.4 = (f32[32,1024]{1,0:T(8,128)S(1)}, f32[32,1024]{1,0:T(8,128)S(1)}, u32[]{:S(2)}, u32[]{:S(2)}) collective-permute-start(f32[32,1024]{1,0:T(8,128)S(1)} %fusion.12), channel_id=1, source_target_pairs={{32,0},{64,32},{96,64},{128,96},{160,128},{192,160},{224,192},{33,... | collective-permute-start | bytes 393224 | tf_op jit(solution)/shard_map/ppermute | solution.py:12
  (8 other events, 17.7 us)
Sparse Core Ops, SparseCore 0:
  10.6 54.3 all-gather.9
  68.8 104.9 all-reduce.4
  177.3 50.7 all-gather.17
  231.4 47.2 all-gather.15
  281.4 50.4 all-gather.11
  335.2 50.5 all-gather.13
  389.4 110.4 all-reduce.6
  503.0 48.6 all-gather.19
  554.3 50.1 all-gather.21
where the time goes:
time: 624 us; the launch traced here: 617 us
  waiting for transfers between devices  240 us (38%)
  blocking collectives  163 us (26%)
  other arithmetic  82 us (13%)
  matrix products  81.8 us (13%)
  local copies, waits for them, and re-layouts  25.7 us (4%)
  between operations  16.7 us (3%)
  starting transfers between devices  7.45 us (1%)
    psum x2, waiting for transfers between devices, combine(): lax.psum(product(factor_pan.T, gain_pan), ('row', 'obs'))  170 us
    dot_general x25, matrix products, product(): jnp.dot(left, right, precision=largest_value, preferred_element_type=jnp....  65.3 us
    unnamed x1, blocking collectives  63.2 us
    another operation x10, other arithmetic, combine(): lower = jnp.linalg.cholesky(system)  47 us
    all_gather x1, blocking collectives, combine(): gain_rows = lax.all_gather(gain_pan, ('row', 'obs'), axis=0, tiled=True)  42.6 us
    all_gather x1, waiting for transfers between devices, per_device(): lax.all_gather(dyn_values, ('row', 'obs'), axis=1, tiled=True)  40.9 us
    all_gather x1, blocking collectives, per_device(): lax.all_gather(offsets, ('row', 'obs'), axis=1, tiled=True)  40.2 us
    another operation x8, other arithmetic, lower_solve(): return lax.linalg.triangular_solve(lower, rhs, left_side=True, lower=True)  30.5 us
  transfers between devices with their start and end apart: 14, of which 6 were waited for; matrix products, arithmetic and copies ran while one was open for 29% of the time, Pallas kernels for 0%

commit v1 on v0

--- a/solution.py
+++ b/solution.py
@@ -67,7 +67,9 @@
     gain_rows = lax.all_gather(gain_pan, ("row", "obs"), axis=0, tiled=True)
     identity = jnp.eye(rank_width, dtype=jnp.float32)
     factor_pan = lax.dynamic_slice_in_dim(own_factor, row_start, panel_rows, 0)
-    system = identity + lax.psum(product(factor_pan.T, gain_pan), ("row", "obs"))
+    system = identity + jnp.sum(
+        lax.all_gather(product(factor_pan.T, gain_pan), ("row", "obs")), axis=0
+    )
     lower = jnp.linalg.cholesky(system)
     carried = product(own_dyn, gain_rows)
     observed = product(prior_dyn.T, own_factor)

time: 624 us -> 542 us (0.87)
  waiting for transfers between devices: 240 us -> 146 us
    psum x2 -> x0, waiting for transfers between devices: 170 us -> none  [combine(): lax.psum(product(factor_pan.T, gain_pan), ('row', 'obs'))]
    all_gather x0 -> x2, waiting for transfers between devices: none -> 82.1 us  [combine(): lax.all_gather(product(factor_pan.T, gain_pan), ('row', 'obs'))]
    all_gather x2, waiting for transfers between devices: 19.4 us -> 0.02 us  [combine(): lax.all_gather(spread_pan, ('row', 'obs'), axis=0, tiled=True)]
    all_gather x1, waiting for transfers between devices: 0.01 us -> 13.2 us  [combine(): gain_rows = lax.all_gather(gain_pan, ('row', 'obs'), axis=0, tiled=True)]
  transfers between devices with their start and end apart: 14 -> 14, of which waited for: 6 -> 6; matrix products, arithmetic and copies ran while one was open for 29% -> 36% of each run, Pallas kernels for 0% -> 0%
where the time goes in v1:
time: 542 us; the launch traced here: 535 us
  blocking collectives  162 us (30%)
  waiting for transfers between devices  146 us (27%)
  matrix products  87.2 us (16%)
  other arithmetic  86.7 us (16%)
  local copies, waits for them, and re-layouts  28.8 us (5%)
  between operations  16.8 us (3%)
  starting transfers between devices  7.44 us (1%)
    all_gather x2, waiting for transfers between devices, combine(): lax.all_gather(product(factor_pan.T, gain_pan), ('row', 'obs'))  82.1 us
    dot_general x25, matrix products, product(): jnp.dot(left, right, precision=largest_value, preferred_element_type=jnp....  66.3 us
    unnamed x1, blocking collectives  61.9 us
    another operation x10, other arithmetic, combine(): lower = jnp.linalg.cholesky(system)  47 us
    all_gather x1, blocking collectives, combine(): gain_rows = lax.all_gather(gain_pan, ('row', 'obs'), axis=0, tiled=True)  42.3 us
    all_gather x1, waiting for transfers between devices, per_device(): lax.all_gather(dyn_values, ('row', 'obs'), axis=1, tiled=True)  40.9 us
    all_gather x1, blocking collectives, per_device(): lax.all_gather(offsets, ('row', 'obs'), axis=1, tiled=True)  40.3 us
    another operation x8, other arithmetic, lower_solve(): return lax.linalg.triangular_solve(lower, rhs, left_side=True, lower=True)  31.8 us
  transfers between devices with their start and end apart: 14, of which 6 were waited for; matrix products, arithmetic and copies ran while one was open for 36% of the time, Pallas kernels for 0%

profile of v1, /device:TPU:1, one launch (start us, length us, event | category | flops | bytes accessed | tf_op | source)
XLA Modules:
  0.0 534.5 jit_solution(10680094058715168137)
XLA Ops:
  8.0 11.5 %all_gather.49 = f32[2,128,256]{2,1,0:T(8,128)S(1)} all-gather(f32[2,32,256]{2,1,0:T(8,128)} %param.16), channel_id=1, replica_groups=mesh['tm'=8,'row'=8,'obs'=4] {'obs'}, dimensions={1}, use_global_device_ids=true | all-gather | bytes 327680 | tf_op jit(solution)/shard_map/all_gather | solution.py:97
  24.0 40.9 %all-gather.14.cloned.1.call-done = f32[2,1024,384]{2,1,0:T(8,128)} async-done(((f32[2,32,384]{2,1,0:T(8,128)}), f32[2,1024,384]{2,1,0:T(8,128)}) %all-gather.14.cloned.1.call-update) | async-done | bytes 3145744 | tf_op jit(solution)/shard_map/all_gather | solution.py:101
  78.1 4.9 convolution_bitcast_fusion.1
  84.7 31.7 %all-gather.28.cloned.1.call-done = f32[4096,128]{1,0:T(8,128)} async-done(((f32[128,128]{1,0:T(8,128)}), f32[4096,128]{1,0:T(8,128)}) %all-gather.28.cloned.1.call-update) | async-done | bytes 2097168 | tf_op jit(solution)/shard_map/all_gather | solution.py:71
  118.2 11.7 %cholesky.60 = f32[128,128]{1,0:T(8,128)S(1)} custom-call(f32[128,128]{1,0:T(8,128)S(1)} %fusion.79), custom_call_target="Cholesky" | custom-call | tf_op jit(solution)/shard_map/jit(cholesky)/cholesky | solution.py:73
  131.3 9.8 %custom-call.31 = f32[1,128,128]{1,2,0:T(8,128)S(1)} custom-call(f32[1,128,128]{2,1,0:T(8,128)S(1)} %fusion.56), custom_call_target="InvertDiagBlocksLowerTriangular" | custom-call | tf_op jit(solution)/shard_map/triangular_solve/custom-call.4 | solution.py:20
  159.2 42.3 %all_gather.52 = f32[1024,128]{1,0:T(8,128)S(1)} all-gather(f32[32,128]{1,0:T(8,128)S(1)} %bitcast.281), channel_id=1, replica_groups=mesh['tm'=8,'row'=8,'obs'=4] {'row','obs'}, dimensions={0}, use_global_device_ids=true | all-gather | bytes 540672 | tf_op jit(solution)/shard_map/all_gather | solution.py:67
  204.9 4.8 fusion.135
  215.3 4.4 collective-permute-done
  221.2 4.8 fusion.53
  231.1 40.3 %all-gather.2 = f32[32,32,2]{1,2,0:T(2,128)S(1)} all-gather(f32[1,32,2]{1,2,0:T(2,128)S(1)} %bitcast.290), channel_id=1, replica_groups=mesh['tm'=8,'row'=8,'obs'=4] {'row','obs'}, dimensions={0}, use_global_device_ids=true | all-gather | bytes 8448 | tf_op jit(solution)/shard_map/all_gather | solution.py:102
  271.5 5.9 %all-gather.3 = f32[4,32,2]{1,2,0:T(2,128)S(1)} all-gather(f32[1,32,2]{1,2,0:T(2,128)S(1)} %bitcast.296), channel_id=1, replica_groups=mesh['tm'=8,'row'=8,'obs'=4] {'obs'}, dimensions={0}, use_global_device_ids=true | all-gather | bytes 1280 | tf_op jit(solution)/shard_map/all_gather | solution.py:98
  279.4 6.7 %fusion.143 = f32[32,1024]{1,0:T(8,128)} fusion(f32[32,1024]{1,0:T(8,128)S(1)} %fusion.12, f32[1024,1024]{1,0:T(8,128)} %all-gather.16.cloned.1.call-done), kind=kOutput, calls=%fused_computation.207 | convolution fusion | flops 402653184 | bytes 4456448 | tf_op jit(solution)/shard_map/dot_general | solution.py:16
  294.2 61.9 %all-reduce.1 = f32[1024]{0:T(1024)S(1)} all-reduce(f32[1024]{0:T(1024)S(1)} %dynamic-update-slice.17), channel_id=1, replica_groups=mesh['tm'=8,'row'=8,'obs'=4] {'row','obs'}, use_global_device_ids=true, to_apply=%add.1 | all-reduce | flops 1024 | bytes 8192
  358.6 5.6 %fusion.142 = f32[256,1024]{1,0:T(8,128)S(1)} fusion(f32[1024,256]{1,0:T(8,128)S(1)} %copy-done.5, f32[1024,1024]{1,0:T(8,128)} %all-gather.18.cloned.1.call-done), kind=kOutput, calls=%fused_computation.206 | convolution fusion | flops 3221225472 | bytes 6291456 | tf_op jit(solution)/shard_map/dot_general | solution.py:16
  364.2 13.2 %all-gather.24.cloned.1.call-done = f32[1024,256]{1,0:T(8,128)} async-done(((f32[32,256]{1,0:T(8,128)}), f32[1024,256]{1,0:T(8,128)}) %all-gather.24.cloned.1.call-update) | async-done | bytes 1048592 | tf_op jit(solution)/shard_map/all_gather | solution.py:67
  377.4 9.4 %fusion.141 = f32[256,1024]{1,0:T(8,128)S(1)} fusion(f32[1024,256]{1,0:T(8,128)} %all-gather.24.cloned.1.call-done, f32[1024,1024]{1,0:T(8,128)} %all-gather.16.cloned.1.call-done), kind=kOutput, calls=%fused_computation.205 | convolution fusion | flops 3221225472 | bytes 6291456 | tf_op jit(solution)/shard_map/dot_general | solution.py:16
  386.9 50.4 %all-gather.30.cloned.1.call-done = f32[8192,256]{1,0:T(8,128)} async-done(((f32[256,256]{1,0:T(8,128)}), f32[8192,256]{1,0:T(8,128)}) %all-gather.30.cloned.1.call-update) | async-done | bytes 8388624 | tf_op jit(solution)/shard_map/all_gather | solution.py:71
  441.4 11.7 %cholesky.115 = f32[128,128]{1,0:T(8,128)S(1)} custom-call(f32[128,128]{1,0:T(8,128)S(1)} %cholesky.141), custom_call_target="Cholesky" | custom-call | tf_op jit(solution)/shard_map/jit(cholesky)/cholesky | solution.py:73
  453.2 9.8 %custom-call.26 = f32[1,128,128]{1,2,0:T(8,128)S(1)} custom-call(f32[1,128,128]{2,1,0:T(8,128)S(1)} %get-tuple-element.62), custom_call_target="InvertDiagBlocksLowerTriangular" | custom-call | tf_op jit(solution)/shard_map/jit(cholesky)/cholesky | solution.py:73
  463.5 11.7 %cholesky.128 = f32[128,128]{1,0:T(8,128)S(1)} custom-call(f32[128,128]{1,0:T(8,128)S(1)} %convolution_subtract_fusion.3), custom_call_target="Cholesky" | custom-call | tf_op jit(solution)/shard_map/jit(cholesky)/cholesky | solution.py:73
  477.9 5.2 while.5
  483.1 20.6 %custom-call.33 = f32[2,128,128]{1,2,0:T(8,128)S(1)} custom-call(f32[2,128,128]{2,1,0:T(8,128)} %get-tuple-element.29), custom_call_target="InvertDiagBlocksLowerTriangular" | custom-call | tf_op jit(solution)/shard_map/triangular_solve/custom-call.5 | solution.py:20
  522.4 5.3 %fusion.11 = f32[1,32,1024]{2,1,0:T(8,128)} fusion(f32[32,1024]{1,0:T(8,128)S(1)} %fusion.12, f32[32,1024]{1,0:T(8,128)} %collective-permute-done.4, f32[32,1024]{1,0:T(8,128)S(1)} %fusion.24, f32[1024,1024]{1,0:T(8,128)} %all-gather.26.cloned.1.call-done, f32[1024,1024]{1,0:T(8,128)} %all-gather.16.cloned.1.call-done, s32[]{:T(128)S(6)} %select_n.93, ...), kind=kOutput, calls=%fused_computation.20 | convolution fusion | flops 402751488 | bytes 4849669 | tf_op jit(solution)/shard_map/dot_general | solution.py:16
  (187 shorter events, 98.4 us)
Async XLA Ops:
  7.2 16.8 %copy-start.23 = (s32[2,8,3]{1,0,2:T(2,128)S(1)}, s32[2,8,3]{1,0,2:T(2,128)}, u32[]{:S(2)}) copy-start(s32[2,8,3]{1,0,2:T(2,128)} %param.11) | copy-start | bytes 580
  7.2 57.8 %all-gather.14.cloned.1.call-start = ((), (), s32[]{:S(2)}) async-start(), calls=%async_computation | async-start | bytes 3244032 | tf_op jit(solution)/shard_map/all_gather | solution.py:101
  7.9 108.5 %all-gather.28.cloned.1.call-start = ((), (), s32[]{:S(2)}) async-start(), calls=%async_computation.7 | async-start | bytes 2162688 | tf_op jit(solution)/shard_map/all_gather | solution.py:71
  23.9 197.3 %all-gather.22.cloned.1.call-start = ((), (), s32[]{:S(2)}) async-start(), calls=%async_computation.4 | async-start | bytes 4325376 | tf_op jit(solution)/shard_map/all_gather | solution.py:80
  83.0 143.5 %all-gather.20.cloned.1.call-start = ((), (), s32[]{:S(2)}) async-start(), calls=%async_computation.3 | async-start | bytes 1081344 | tf_op jit(solution)/shard_map/all_gather | solution.py:128
  84.7 63.0 %copy-start.10 = (f32[8,128,128]{2,1,0:T(8,128)}, f32[8,128,128]{2,1,0:T(8,128)S(1)}, u32[]{:S(2)}) copy-start(f32[8,128,128]{2,1,0:T(8,128)S(1)} %copy.52) | copy-start | bytes 1572868
  84.7 68.7 %copy-start.14 = (f32[32,128]{1,0:T(8,128)}, f32[32,128]{1,0:T(8,128)S(1)}, u32[]{:S(2)}) copy-start(f32[32,128]{1,0:T(8,128)S(1)} %constant_dynamic-slice_fusion.1) | copy-start | bytes 49156
  153.4 5.1 collective-permute-start.1
  159.1 120.3 %all-gather.16.cloned.1.call-start = ((), (), s32[]{:S(2)}) async-start(), calls=%async_computation.1 | async-start | bytes 4325376 | tf_op jit(solution)/shard_map/all_gather | solution.py:127
  213.8 17.3 %copy-start.22 = (f32[2,32]{1,0:T(2,128)S(1)}, f32[2,32]{1,0:T(2,128)}, u32[]{:S(2)}) copy-start(f32[2,32]{1,0:T(2,128)} %param.13) | copy-start | bytes 772
  213.8 57.7 %copy-start.25 = (f32[2,32]{1,0:T(2,128)S(1)}, f32[2,32]{1,0:T(2,128)}, u32[]{:S(2)}) copy-start(f32[2,32]{1,0:T(2,128)} %param.17) | copy-start | bytes 772
  213.8 5.8 %collective-permute-start = (f32[32,1024]{1,0:T(8,128)S(1)}, f32[32,1024]{1,0:T(8,128)S(1)}, u32[]{:S(2)}, u32[]{:S(2)}) collective-permute-start(f32[32,1024]{1,0:T(8,128)S(1)} %fusion.6), channel_id=1, source_target_pairs={{32,0},{64,32},{96,64},{128,96},{160,128},{192,160},{224,192},{33,... | collective-permute-start | bytes 393224 | tf_op jit(solution)/shard_map/ppermute | solution.py:12
  220.4 138.2 %all-gather.18.cloned.1.call-start = ((), (), s32[]{:S(2)}) async-start(), calls=%async_computation.2 | async-start | bytes 4325376 | tf_op jit(solution)/shard_map/all_gather | solution.py:126
  220.9 156.4 %all-gather.24.cloned.1.call-start = ((), (), s32[]{:S(2)}) async-start(), calls=%async_computation.5 | async-start | bytes 1081344 | tf_op jit(solution)/shard_map/all_gather | solution.py:67
  226.0 60.7 %copy-start.26 = (u32[256]{0:T(256)S(1)}, u32[256]{0:T(256)}, u32[]{:S(2)}) copy-start(u32[256]{0:T(256)} %constant.218) | copy-start | bytes 3076
  226.5 129.6 %copy-start.5 = (f32[1024,256]{1,0:T(8,128)S(1)}, f32[1024,256]{1,0:T(8,128)}, u32[]{:S(2)}) copy-start(f32[1024,256]{1,0:T(8,128)} %all-gather.20.cloned.1.call-done) | copy-start | bytes 3145732
  229.1 208.2 %all-gather.30.cloned.1.call-start = ((), (), s32[]{:S(2)}) async-start(), calls=%async_computation.8 | async-start | bytes 8650752 | tf_op jit(solution)/shard_map/all_gather | solution.py:71
  231.1 291.4 %all-gather.26.cloned.1.call-start = ((), (), s32[]{:S(2)}) async-start(), calls=%async_computation.6 | async-start | bytes 4325376 | tf_op jit(solution)/shard_map/all_gather | solution.py:80
  287.9 98.9 %copy-start.24 = (f32[128]{0:T(128)}, f32[128]{0:T(128)S(1)}, u32[]{:S(2)}) copy-start(f32[128]{0:T(128)S(1)} %slice_bitcast_fusion.11) | copy-start | bytes 1540
  288.1 98.8 %copy-start.21 = (f32[1,128]{1,0:T(1,128)}, f32[1,128]{1,0:T(1,128)S(1)}, u32[]{:S(2)}) copy-start(f32[1,128]{1,0:T(1,128)S(1)} %fusion.72) | copy-start | bytes 1540
  288.1 68.6 %collective-permute-start.2 = (f32[256]{0:T(256)S(1)}, f32[256]{0:T(256)S(1)}, u32[]{:S(2)}, u32[]{:S(2)}) collective-permute-start(f32[256]{0:T(256)S(1)} %pad_maximum_fusion.5), channel_id=1, source_target_pairs={{32,0},{64,32},{96,64},{128,96},{160,128},{192,160},{224,192},{33,... | collective-permute-start | bytes 3080 | tf_op jit(solution)/shard_map/ppermute | solution.py:12
  292.1 228.7 %collective-permute-start.3 = (f32[32]{0:T(128)}, f32[32]{0:T(128)}, u32[]{:S(2)}, u32[]{:S(2)}) collective-permute-start(f32[32]{0:T(128)} %fusion.16), channel_id=1, source_target_pairs={{32,0},{64,32},{96,64},{128,96},{160,128},{192,160},{224,192},{33,... | collective-permute-start | bytes 392 | tf_op jit(solution)/shard_map/ppermute | solution.py:12
  357.3 165.2 %collective-permute-start.4 = (f32[32,1024]{1,0:T(8,128)S(1)}, f32[32,1024]{1,0:T(8,128)}, u32[]{:S(2)}, u32[]{:S(2)}) collective-permute-start(f32[32,1024]{1,0:T(8,128)S(1)} %fusion.12), channel_id=1, source_target_pairs={{32,0},{64,32},{96,64},{128,96},{160,128},{192,160},{224,192},{33,... | collective-permute-start | bytes 393224 | tf_op jit(solution)/shard_map/ppermute | solution.py:12
  437.3 40.6 %copy-start.27 = (s32[2]{0:T(128)S(1)}, s32[2]{0:T(128)}, u32[]{:S(2)}) copy-start(s32[2]{0:T(128)} %iota_multiply_fusion) | copy-start | bytes 28
  (18 other events, 110.3 us)
Sparse Core Ops, SparseCore 0:
  10.6 54.3 all-gather.13
  68.1 48.2 all-gather.27
  119.5 50.5 all-gather.21
  173.1 47.3 all-gather.19
  222.8 50.4 all-gather.15
  276.4 50.5 all-gather.17
  330.1 47.2 all-gather.23
  379.9 57.2 all-gather.29
  439.8 51.3 all-gather.25
